TPU v7x, 512 devices: a whole 4x8x8 slice. The times are simulated.
512 devices in a mesh: row: 64 (over x, y, z_hi), col: 8 (over z_lo, core).
Axes of the slice: x: 4, y: 8, z: 8 (z_hi: 2, z_lo: 4; z = z_hi * 4 + z_lo), core: 2. Of those that a mesh axis runs over, the one named last changes fastest.
Arguments:
- features: float32 [16384, 512], P('row', 'col'), may hold values from -20 to 20
- adj_values: bfloat16 [256, 64, 4096], P('row', 'col'), may hold values from 0 to 0.0078125
- adj_cols: int32 [256, 64], P('row', 'col'), may hold values from 0 to 255, as said below
- adj_count: int32 [256], P('row'), may hold values from 16 to 64, as said below
Outputs:
- hop_one: float32 [16384, 512], P('row', 'col')
- hop_two: float32 [16384, 512], P('row', 'col')
Inputs may be any that keep to these rules, and one draw needn't show every extreme that they name: `adj_cols`: within one row block the column blocks of all 64 slots are distinct. `adj_count`: some row block has all 64 slots live.
All inputs are finite; a program needn't handle non-finite values.
Results may differ from a plain program's by a relative error of at most 0.0003.
Values may be sent and summed in bfloat16 or wider, within the bound.
A program may use at most 128 MiB of HBM per device.

v0:
```python
import jax
import jax.numpy as jnp
from jax import lax
from jax.sharding import PartitionSpec as P

BLK = 64


def masked_tiles(tile_all, adj_count):
    slot_total = tile_all.shape[1]
    slot_ids = jnp.arange(slot_total, dtype=jnp.int32)
    live_mask = (slot_ids[None, :] < adj_count[:, None]).astype(jnp.float32)
    weights = tile_all.astype(jnp.float32).reshape(tile_all.shape[0], slot_total, BLK, BLK)
    return weights * live_mask[:, :, None, None]


def propagate(slab, weights, col_all):
    feat_width = slab.shape[1]
    blocks = slab.reshape(-1, BLK, feat_width)

    def single(record):
        weight_set, col_ids = record
        picked = blocks[col_ids]
        return jnp.einsum("kij,kjf->if", weight_set, picked, precision=lax.Precision.HIGHEST)

    result = lax.map(single, (weights, col_all))
    return result.reshape(-1, feat_width)


def local(features, adj_values, adj_cols, adj_count):
    tile_all, col_all = (
        lax.all_gather(adj_values, "col", axis=1, tiled=True),
        lax.all_gather(adj_cols, "col", axis=1, tiled=True),
    )
    weights = masked_tiles(tile_all, adj_count)
    slab = lax.all_gather(features, "row", axis=0, tiled=True)
    hop_one = propagate(slab, weights, col_all)
    second_slab = lax.all_gather(hop_one, "row", axis=0, tiled=True)
    hop_two = propagate(second_slab, weights, col_all)
    return (hop_one, hop_two)


def solution(mesh):
    in_specs = (P("row", "col"), P("row", "col", None), P("row", "col"), P("row"))
    out_specs = (P("row", "col"), P("row", "col"))
    return jax.shard_map(local, mesh=mesh, in_specs=in_specs, out_specs=out_specs, check_vma=False)
```

profile of v0, /device:TPU:2, one launch (start us, length us, event | category | flops | bytes accessed | tf_op | source)
XLA Modules:
  0.0 467.1 jit_solution(14740028736777230822)
XLA Ops:
  7.2 0.0 all-gather.5.cloned.1.call-start
  7.2 0.7 all-gather.5.cloned.1.call-update
  7.9 0.0 all-gather.7.cloned.1.call-start
  7.9 0.7 all-gather.7.cloned.1.call-update
  8.6 0.0 all-gather.9.cloned.1.call-start
  8.7 15.2 %all-gather = s32[8,8,4]{1,2,0:T(4,128)S(1)} all-gather(s32[1,8,4]{1,2,0:T(4,128)} %bitcast.70), channel_id=1, replica_groups=mesh['row'=64,'col'=8] {'col'}, dimensions={0}, use_global_device_ids=true | all-gather | bytes 1152 | tf_op jit(solution)/shard_map/all_gather | solution.py:33
  23.9 0.1 reshape.125
  23.9 0.7 fusion.34
  24.7 31.9 %all-gather.5.cloned.1.call-done = bf16[4,64,4096]{2,1,0:T(8,128)(2,1)} async-done(((bf16[4,8,4096]{2,1,0:T(8,128)(2,1)}), bf16[4,64,4096]{2,1,0:T(8,128)(2,1)}) %all-gather.5.cloned.1.call-update) | async-done | bytes 2097168 | tf_op jit(solution)/shard_map/all_gather | solution.py:32
  56.6 7.0 %reshape.107 = f32[4,64,64,64]{3,2,1,0:T(8,128)} reshape(bf16[4,64,4096]{2,1,0:T(8,128)(2,1)} %all-gather.5.cloned.1.call-done) | data formatting | bytes 6291456 | tf_op jit(solution)/shard_map/reshape | solution.py:13
  63.6 7.2 %broadcast_multiply_fusion = f32[4,64,64,64]{3,2,1,0:T(8,128)} fusion(f32[4,64,64,64]{3,2,1,0:T(8,128)} %reshape.107, f32[4,64]{1,0:T(4,128)S(1)} %fusion.34), kind=kLoop, calls=%fused_computation.26 | loop fusion | flops 1048576 | bytes 8389632 | tf_op jit(solution)/shard_map/mul | solution.py:14
  70.8 9.0 %copy.25 = f32[4,64,64,64]{1,2,3,0:T(8,128)} copy(f32[4,64,64,64]{3,2,1,0:T(8,128)} %broadcast_multiply_fusion) | data formatting | bytes 8388608 | tf_op jit(solution)/shard_map/while | solution.py:26
  79.8 141.0 %all-gather.7.cloned.1.call-done = f32[16384,64]{0,1:T(8,128)} async-done(((f32[256,64]{0,1:T(8,128)}), f32[16384,64]{0,1:T(8,128)}) %all-gather.7.cloned.1.call-update) | async-done | bytes 4194320 | tf_op jit(solution)/shard_map/all_gather | solution.py:36
  220.8 6.9 %copy.24 = f32[16384,64]{1,0:T(8,128)} copy(f32[16384,64]{0,1:T(8,128)} %all-gather.7.cloned.1.call-done) | data formatting | bytes 8388608 | tf_op jit(solution)/shard_map/all_gather | solution.py:36
  227.7 35.2 %while.20 = (s32[]{:T(128)}, f32[4,64,64]{2,1,0:T(8,128)S(1)}, f32[4,64,64,64]{1,2,3,0:T(8,128)}, s32[4,64]{1,0:T(4,128)S(1)}, f32[256,64,64]{2,1,0:T(8,128)}, /*index=5*/s32[]{:T(128)}) while((s32[]{:T(128)}, f32[4,64,64]{2,1,0:T(8,128)S(1)}, f32[4,64,64,64]{1,2,3,0:T(8,128)}, s32[4,64]{1,0:T(4,128)S(1)}, f32[256,64,64]{2,1,0:T(8,128)}, ...), condition=%wide.region_1.2_spmd, body=%wide.region_0.1_spmd.sunk | while | flops 201327808 | bytes 6330441 | solution.py:26
  227.7 4.1 gather_fusion
  231.8 4.7 %fusion.46 = f32[4,64,64]{2,1,0:T(8,128)S(1)} fusion(f32[4,64,64]{2,1,0:T(8,128)S(1)} %get-tuple-element.172, s32[]{:T(128)} %get-tuple-element.171, f32[64,64,64]{2,1,0:T(8,128)S(1)} %gather_fusion, f32[4,64,64,64]{1,2,3,0:T(8,128)} %get-tuple-element.179), kind=kOutput, calls=%fused_computation.7.clone.1 | convolution fusion | flops 201326592 | bytes 4228096 | tf_op jit(solution)/shard_map/while/body/eval_jaxpr/kij,kjf->if/dot_general | solution.py:24
  236.5 4.1 gather_fusion
  240.6 4.7 %fusion.46 = f32[4,64,64]{2,1,0:T(8,128)S(1)} fusion(f32[4,64,64]{2,1,0:T(8,128)S(1)} %get-tuple-element.172, s32[]{:T(128)} %get-tuple-element.171, f32[64,64,64]{2,1,0:T(8,128)S(1)} %gather_fusion, f32[4,64,64,64]{1,2,3,0:T(8,128)} %get-tuple-element.179), kind=kOutput, calls=%fused_computation.7.clone.1 | convolution fusion | flops 201326592 | bytes 4228096 | tf_op jit(solution)/shard_map/while/body/eval_jaxpr/kij,kjf->if/dot_general | solution.py:24
  245.3 4.1 gather_fusion
  249.4 4.7 %fusion.46 = f32[4,64,64]{2,1,0:T(8,128)S(1)} fusion(f32[4,64,64]{2,1,0:T(8,128)S(1)} %get-tuple-element.172, s32[]{:T(128)} %get-tuple-element.171, f32[64,64,64]{2,1,0:T(8,128)S(1)} %gather_fusion, f32[4,64,64,64]{1,2,3,0:T(8,128)} %get-tuple-element.179), kind=kOutput, calls=%fused_computation.7.clone.1 | convolution fusion | flops 201326592 | bytes 4228096 | tf_op jit(solution)/shard_map/while/body/eval_jaxpr/kij,kjf->if/dot_general | solution.py:24
  254.1 4.1 gather_fusion
  258.2 4.7 %fusion.46 = f32[4,64,64]{2,1,0:T(8,128)S(1)} fusion(f32[4,64,64]{2,1,0:T(8,128)S(1)} %get-tuple-element.172, s32[]{:T(128)} %get-tuple-element.171, f32[64,64,64]{2,1,0:T(8,128)S(1)} %gather_fusion, f32[4,64,64,64]{1,2,3,0:T(8,128)} %get-tuple-element.179), kind=kOutput, calls=%fused_computation.7.clone.1 | convolution fusion | flops 201326592 | bytes 4228096 | tf_op jit(solution)/shard_map/while/body/eval_jaxpr/kij,kjf->if/dot_general | solution.py:24
  262.9 0.7 copy.30
  263.6 0.0 all-gather.9.cloned.1.call-update
  263.6 154.2 %all-gather.9.cloned.1.call-done = f32[16384,64]{0,1:T(8,128)} async-done(((f32[256,64]{0,1:T(8,128)}), f32[16384,64]{0,1:T(8,128)}) %all-gather.9.cloned.1.call-update) | async-done | bytes 4194320 | tf_op jit(solution)/shard_map/all_gather | solution.py:38
  417.8 6.9 %copy.31 = f32[16384,64]{1,0:T(8,128)} copy(f32[16384,64]{0,1:T(8,128)} %all-gather.9.cloned.1.call-done) | data formatting | bytes 8388608 | tf_op jit(solution)/shard_map/while | solution.py:26
  424.7 35.2 %while.21 = (s32[]{:T(128)}, f32[4,64,64]{2,1,0:T(8,128)S(1)}, f32[4,64,64,64]{1,2,3,0:T(8,128)}, s32[4,64]{1,0:T(4,128)S(1)}, f32[256,64,64]{2,1,0:T(8,128)}, /*index=5*/s32[]{:T(128)}) while((s32[]{:T(128)}, f32[4,64,64]{2,1,0:T(8,128)S(1)}, f32[4,64,64,64]{1,2,3,0:T(8,128)}, s32[4,64]{1,0:T(4,128)S(1)}, f32[256,64,64]{2,1,0:T(8,128)}, ...), condition=%wide.region_3.4_spmd, body=%wide.region_2.3_spmd.sunk | while | flops 201327808 | bytes 6330441 | solution.py:26
  424.7 4.1 gather_fusion.1
  428.8 4.7 %fusion.50 = f32[4,64,64]{2,1,0:T(8,128)S(1)} fusion(f32[4,64,64]{2,1,0:T(8,128)S(1)} %get-tuple-element.190, s32[]{:T(128)} %get-tuple-element.189, f32[64,64,64]{2,1,0:T(8,128)S(1)} %gather_fusion.1, f32[4,64,64,64]{1,2,3,0:T(8,128)} %get-tuple-element.197), kind=kOutput, calls=%fused_computation.19.clone.1 | convolution fusion | flops 201326592 | bytes 4228096 | tf_op jit(solution)/shard_map/while/body/eval_jaxpr/kij,kjf->if/dot_general | solution.py:24
  433.5 4.1 gather_fusion.1
  437.6 4.7 %fusion.50 = f32[4,64,64]{2,1,0:T(8,128)S(1)} fusion(f32[4,64,64]{2,1,0:T(8,128)S(1)} %get-tuple-element.190, s32[]{:T(128)} %get-tuple-element.189, f32[64,64,64]{2,1,0:T(8,128)S(1)} %gather_fusion.1, f32[4,64,64,64]{1,2,3,0:T(8,128)} %get-tuple-element.197), kind=kOutput, calls=%fused_computation.19.clone.1 | convolution fusion | flops 201326592 | bytes 4228096 | tf_op jit(solution)/shard_map/while/body/eval_jaxpr/kij,kjf->if/dot_general | solution.py:24
  442.3 4.1 gather_fusion.1
  446.4 4.7 %fusion.50 = f32[4,64,64]{2,1,0:T(8,128)S(1)} fusion(f32[4,64,64]{2,1,0:T(8,128)S(1)} %get-tuple-element.190, s32[]{:T(128)} %get-tuple-element.189, f32[64,64,64]{2,1,0:T(8,128)S(1)} %gather_fusion.1, f32[4,64,64,64]{1,2,3,0:T(8,128)} %get-tuple-element.197), kind=kOutput, calls=%fused_computation.19.clone.1 | convolution fusion | flops 201326592 | bytes 4228096 | tf_op jit(solution)/shard_map/while/body/eval_jaxpr/kij,kjf->if/dot_general | solution.py:24
  451.1 4.1 gather_fusion.1
  455.2 4.7 %fusion.50 = f32[4,64,64]{2,1,0:T(8,128)S(1)} fusion(f32[4,64,64]{2,1,0:T(8,128)S(1)} %get-tuple-element.190, s32[]{:T(128)} %get-tuple-element.189, f32[64,64,64]{2,1,0:T(8,128)S(1)} %gather_fusion.1, f32[4,64,64,64]{1,2,3,0:T(8,128)} %get-tuple-element.197), kind=kOutput, calls=%fused_computation.19.clone.1 | convolution fusion | flops 201326592 | bytes 4228096 | tf_op jit(solution)/shard_map/while/body/eval_jaxpr/kij,kjf->if/dot_general | solution.py:24
  459.8 0.7 copy.32
  (19 shorter events, 0.1 us)
Async XLA Ops:
  7.2 49.4 %all-gather.5.cloned.1.call-start = ((), (), s32[]{:S(2)}) async-start(), calls=%async_computation | async-start | bytes 2359296 | tf_op jit(solution)/shard_map/all_gather | solution.py:32
  7.9 212.9 %all-gather.7.cloned.1.call-start = ((), (), s32[]{:S(2)}) async-start(), calls=%async_computation.1 | async-start | bytes 4259840 | tf_op jit(solution)/shard_map/all_gather | solution.py:36
  8.6 409.1 %all-gather.9.cloned.1.call-start = ((), (), s32[]{:S(2)}) async-start(), calls=%async_computation.2 | async-start | bytes 4259840 | tf_op jit(solution)/shard_map/all_gather | solution.py:38
Sparse Core Ops, SparseCore 0:
  10.1 46.4 all-gather.4
  60.9 159.8 all-gather.6
  263.7 154.0 all-gather.8
where the time goes:
time: 468 us; the launch traced here: 467 us
  waiting for transfers between devices  328 us (70%)
  local copies, waits for them, and re-layouts  63.7 us (14%)
  matrix products  37.5 us (8%)
  blocking collectives  15.2 us (3%)
  between operations  13.8 us (3%)
  other arithmetic  8.08 us (2%)
    all_gather x1, waiting for transfers between devices, local(): second_slab = lax.all_gather(hop_one, 'row', axis=0, tiled=True)  154 us
    all_gather x1, waiting for transfers between devices, local(): slab = lax.all_gather(features, 'row', axis=0, tiled=True)  141 us
    dot_general x8, matrix products, single(): jnp.einsum('kij,kjf->if', weight_set, picked, precision=lax.Precision.HIG...  37.5 us
    gather x8, local copies, waits for them, and re-layouts, single(): picked = blocks[col_ids]  32.5 us
    all_gather x1, waiting for transfers between devices, local(): lax.all_gather(adj_values, 'col', axis=1, tiled=True)  31.9 us
    while x2, local copies, waits for them, and re-layouts, propagate(): result = lax.map(single, (weights, col_all))  15.9 us
    all_gather x1, blocking collectives, local(): lax.all_gather(adj_cols, 'col', axis=1, tiled=True)  15.2 us
  transfers between devices with their start and end apart: 3, of which 3 were waited for; matrix products, arithmetic and copies ran while one was open for 5% of the time, Pallas kernels for 0%

commit v1 on v0

--- a/solution.py
+++ b/solution.py
@@ -29,7 +29,9 @@
 
 def local(features, adj_values, adj_cols, adj_count):
     tile_all, col_all = (
-        lax.all_gather(adj_values, "col", axis=1, tiled=True),
+        jnp.concatenate(
+            lax.all_to_all(jnp.stack([adj_values] * lax.axis_size("col")), "col", 0, 0), axis=1
+        ),
         lax.all_gather(adj_cols, "col", axis=1, tiled=True),
     )
     weights = masked_tiles(tile_all, adj_count)

time: 468 us -> 425 us (0.908)
  waiting for transfers between devices: 328 us -> 232 us
  blocking collectives: 15.2 us -> 55.8 us
  starting transfers between devices: 0.11 us -> 7.47 us
  local copies, waits for them, and re-layouts: 63.7 us -> 69.3 us
    all_gather x1, waiting for transfers between devices: 141 us -> 76.9 us  [local(): slab = lax.all_gather(features, 'row', axis=0, tiled=True)]
    all_gather x1, blocking collectives: 15.2 us -> 55.8 us  [local(): lax.all_gather(adj_cols, 'col', axis=1, tiled=True)]
    all_gather x1 -> x0, waiting for transfers between devices: 31.9 us -> none  [local(): lax.all_gather(adj_values, 'col', axis=1, tiled=True)]
    convert_element_type x0 -> x2, local copies, waits for them, and re-layouts: none -> 10.1 us  [masked_tiles(): tile_all.astype(jnp.float32)]
    all_to_all x0 -> x1, starting transfers between devices: none -> 7.4 us  [local(): lax.all_to_all(jnp.stack([adj_values] * lax.axis_size('col')), 'col', 0, 0)]
    reshape x1 -> x0, local copies, waits for them, and re-layouts: 7 us -> none  [masked_tiles(): tile_all.astype(jnp.float32)]
  transfers between devices with their start and end apart: 3 -> 3, of which waited for: 3 -> 2; matrix products, arithmetic and copies ran while one was open for 5% -> 7% of each run, Pallas kernels for 0% -> 0%
where the time goes in v1:
time: 425 us; the launch traced here: 424 us
  waiting for transfers between devices  232 us (55%)
  local copies, waits for them, and re-layouts  69.3 us (16%)
  blocking collectives  55.8 us (13%)
  matrix products  37.5 us (9%)
  between operations  14.1 us (3%)
  other arithmetic  7.95 us (2%)
  starting transfers between devices  7.47 us (2%)
    all_gather x1, waiting for transfers between devices, local(): second_slab = lax.all_gather(hop_one, 'row', axis=0, tiled=True)  154 us
    all_gather x1, waiting for transfers between devices, local(): slab = lax.all_gather(features, 'row', axis=0, tiled=True)  76.9 us
    all_gather x1, blocking collectives, local(): lax.all_gather(adj_cols, 'col', axis=1, tiled=True)  55.8 us
    dot_general x8, matrix products, single(): jnp.einsum('kij,kjf->if', weight_set, picked, precision=lax.Precision.HIG...  37.5 us
    gather x8, local copies, waits for them, and re-layouts, single(): picked = blocks[col_ids]  32.5 us
    while x2, local copies, waits for them, and re-layouts, propagate(): result = lax.map(single, (weights, col_all))  15.8 us
    convert_element_type x2, local copies, waits for them, and re-layouts, masked_tiles(): tile_all.astype(jnp.float32)  10.1 us
  transfers between devices with their start and end apart: 3, of which 2 were waited for; matrix products, arithmetic and copies ran while one was open for 7% of the time, Pallas kernels for 0%

profile of v1, /device:TPU:2, one launch (start us, length us, event | category | flops | bytes accessed | tf_op | source)
XLA Modules:
  0.0 424.1 jit_solution(17703573662531840142)
XLA Ops:
  7.2 0.0 all-gather.4.cloned.1.call-start
  7.2 0.7 all-gather.4.cloned.1.call-update
  7.9 2.5 stack.2
  10.4 0.0 copy-start
  10.4 0.0 copy-start.1
  10.4 7.4 %all-to-all-start = ((bf16[8,4,8,4096]{3,2,1,0:T(8,128)(2,1)}), bf16[8,4,8,4096]{3,2,1,0:T(8,128)(2,1)S(1)}, u32[]{:S(2)}, u32[]{:S(2)}) async-start(bf16[8,4,8,4096]{3,2,1,0:T(8,128)(2,1)} %stack.2), calls=%async_computation | async-start | bytes 4194304 | tf_op jit(solution)/shard_map/all_to_all | solution.py:33
  17.8 0.0 all-gather.6.cloned.1.call-start
  17.9 0.0 copy-done
  17.9 55.8 %all-gather = s32[8,8,4]{1,2,0:T(4,128)S(1)} all-gather(s32[1,8,4]{1,2,0:T(4,128)S(1)} %bitcast.74), channel_id=1, replica_groups=mesh['row'=64,'col'=8] {'col'}, dimensions={0}, use_global_device_ids=true | all-gather | bytes 1152 | tf_op jit(solution)/shard_map/all_gather | solution.py:35
  73.7 0.1 reshape.124
  73.7 0.0 copy-done.1
  73.7 0.1 fusion.34
  73.8 0.0 all-to-all-done
  73.8 0.5 convert_bitcast_fusion
  74.3 2.2 copy.23
  76.6 7.8 %reshape.106 = f32[4,64,64,64]{3,2,1,0:T(8,128)} reshape(f32[4,8,8,4096]{3,2,1,0:T(8,128)} %copy.23) | data formatting | bytes 8388608 | tf_op jit(solution)/shard_map/convert_element_type | solution.py:13
  84.4 7.3 %broadcast_multiply_fusion = f32[4,64,64,64]{3,2,1,0:T(8,128)} fusion(f32[4,64,64,64]{3,2,1,0:T(8,128)} %reshape.106, f32[4,64]{1,0:T(4,128)S(1)} %fusion.34), kind=kLoop, calls=%fused_computation.27 | loop fusion | flops 1048576 | bytes 8389632 | tf_op jit(solution)/shard_map/mul | solution.py:14
  91.7 9.0 %copy.26 = f32[4,64,64,64]{1,2,3,0:T(8,128)} copy(f32[4,64,64,64]{3,2,1,0:T(8,128)} %broadcast_multiply_fusion) | data formatting | bytes 8388608 | tf_op jit(solution)/shard_map/while | solution.py:26
  100.7 76.9 %all-gather.4.cloned.1.call-done = f32[16384,64]{0,1:T(8,128)} async-done(((f32[256,64]{0,1:T(8,128)}), f32[16384,64]{0,1:T(8,128)}) %all-gather.4.cloned.1.call-update) | async-done | bytes 4194320 | tf_op jit(solution)/shard_map/all_gather | solution.py:38
  177.5 6.8 %copy.25 = f32[16384,64]{1,0:T(8,128)} copy(f32[16384,64]{0,1:T(8,128)} %all-gather.4.cloned.1.call-done) | data formatting | bytes 8388608 | tf_op jit(solution)/shard_map/all_gather | solution.py:38
  184.4 35.2 %while.20 = (s32[]{:T(128)}, f32[4,64,64]{2,1,0:T(8,128)S(1)}, f32[4,64,64,64]{1,2,3,0:T(8,128)}, s32[4,64]{1,0:T(4,128)S(1)}, f32[256,64,64]{2,1,0:T(8,128)}, /*index=5*/s32[]{:T(128)}) while((s32[]{:T(128)}, f32[4,64,64]{2,1,0:T(8,128)S(1)}, f32[4,64,64,64]{1,2,3,0:T(8,128)}, s32[4,64]{1,0:T(4,128)S(1)}, f32[256,64,64]{2,1,0:T(8,128)}, ...), condition=%wide.region_1.2_spmd, body=%wide.region_0.1_spmd.sunk | while | flops 201327808 | bytes 6330441 | solution.py:26
  184.4 4.1 gather_fusion
  188.5 4.7 %fusion.46 = f32[4,64,64]{2,1,0:T(8,128)S(1)} fusion(f32[4,64,64]{2,1,0:T(8,128)S(1)} %get-tuple-element.172, s32[]{:T(128)} %get-tuple-element.171, f32[64,64,64]{2,1,0:T(8,128)S(1)} %gather_fusion, f32[4,64,64,64]{1,2,3,0:T(8,128)} %get-tuple-element.179), kind=kOutput, calls=%fused_computation.7.clone.1 | convolution fusion | flops 201326592 | bytes 4228096 | tf_op jit(solution)/shard_map/while/body/eval_jaxpr/kij,kjf->if/dot_general | solution.py:24
  193.2 4.1 gather_fusion
  197.3 4.7 %fusion.46 = f32[4,64,64]{2,1,0:T(8,128)S(1)} fusion(f32[4,64,64]{2,1,0:T(8,128)S(1)} %get-tuple-element.172, s32[]{:T(128)} %get-tuple-element.171, f32[64,64,64]{2,1,0:T(8,128)S(1)} %gather_fusion, f32[4,64,64,64]{1,2,3,0:T(8,128)} %get-tuple-element.179), kind=kOutput, calls=%fused_computation.7.clone.1 | convolution fusion | flops 201326592 | bytes 4228096 | tf_op jit(solution)/shard_map/while/body/eval_jaxpr/kij,kjf->if/dot_general | solution.py:24
  202.0 4.1 gather_fusion
  206.1 4.7 %fusion.46 = f32[4,64,64]{2,1,0:T(8,128)S(1)} fusion(f32[4,64,64]{2,1,0:T(8,128)S(1)} %get-tuple-element.172, s32[]{:T(128)} %get-tuple-element.171, f32[64,64,64]{2,1,0:T(8,128)S(1)} %gather_fusion, f32[4,64,64,64]{1,2,3,0:T(8,128)} %get-tuple-element.179), kind=kOutput, calls=%fused_computation.7.clone.1 | convolution fusion | flops 201326592 | bytes 4228096 | tf_op jit(solution)/shard_map/while/body/eval_jaxpr/kij,kjf->if/dot_general | solution.py:24
  210.8 4.1 gather_fusion
  214.9 4.7 %fusion.46 = f32[4,64,64]{2,1,0:T(8,128)S(1)} fusion(f32[4,64,64]{2,1,0:T(8,128)S(1)} %get-tuple-element.172, s32[]{:T(128)} %get-tuple-element.171, f32[64,64,64]{2,1,0:T(8,128)S(1)} %gather_fusion, f32[4,64,64,64]{1,2,3,0:T(8,128)} %get-tuple-element.179), kind=kOutput, calls=%fused_computation.7.clone.1 | convolution fusion | flops 201326592 | bytes 4228096 | tf_op jit(solution)/shard_map/while/body/eval_jaxpr/kij,kjf->if/dot_general | solution.py:24
  219.6 0.7 copy.31
  220.3 0.0 all-gather.6.cloned.1.call-update
  220.3 154.2 %all-gather.6.cloned.1.call-done = f32[16384,64]{0,1:T(8,128)} async-done(((f32[256,64]{0,1:T(8,128)}), f32[16384,64]{0,1:T(8,128)}) %all-gather.6.cloned.1.call-update) | async-done | bytes 4194320 | tf_op jit(solution)/shard_map/all_gather | solution.py:40
  374.5 6.8 %copy.32 = f32[16384,64]{1,0:T(8,128)} copy(f32[16384,64]{0,1:T(8,128)} %all-gather.6.cloned.1.call-done) | data formatting | bytes 8388608 | tf_op jit(solution)/shard_map/while | solution.py:26
  381.4 35.2 %while.21 = (s32[]{:T(128)}, f32[4,64,64]{2,1,0:T(8,128)S(1)}, f32[4,64,64,64]{1,2,3,0:T(8,128)}, s32[4,64]{1,0:T(4,128)S(1)}, f32[256,64,64]{2,1,0:T(8,128)}, /*index=5*/s32[]{:T(128)}) while((s32[]{:T(128)}, f32[4,64,64]{2,1,0:T(8,128)S(1)}, f32[4,64,64,64]{1,2,3,0:T(8,128)}, s32[4,64]{1,0:T(4,128)S(1)}, f32[256,64,64]{2,1,0:T(8,128)}, ...), condition=%wide.region_3.4_spmd, body=%wide.region_2.3_spmd.sunk | while | flops 201327808 | bytes 6330441 | solution.py:26
  381.4 4.1 gather_fusion.1
  385.5 4.7 %fusion.50 = f32[4,64,64]{2,1,0:T(8,128)S(1)} fusion(f32[4,64,64]{2,1,0:T(8,128)S(1)} %get-tuple-element.190, s32[]{:T(128)} %get-tuple-element.189, f32[64,64,64]{2,1,0:T(8,128)S(1)} %gather_fusion.1, f32[4,64,64,64]{1,2,3,0:T(8,128)} %get-tuple-element.197), kind=kOutput, calls=%fused_computation.19.clone.1 | convolution fusion | flops 201326592 | bytes 4228096 | tf_op jit(solution)/shard_map/while/body/eval_jaxpr/kij,kjf->if/dot_general | solution.py:24
  390.2 4.1 gather_fusion.1
  394.3 4.7 %fusion.50 = f32[4,64,64]{2,1,0:T(8,128)S(1)} fusion(f32[4,64,64]{2,1,0:T(8,128)S(1)} %get-tuple-element.190, s32[]{:T(128)} %get-tuple-element.189, f32[64,64,64]{2,1,0:T(8,128)S(1)} %gather_fusion.1, f32[4,64,64,64]{1,2,3,0:T(8,128)} %get-tuple-element.197), kind=kOutput, calls=%fused_computation.19.clone.1 | convolution fusion | flops 201326592 | bytes 4228096 | tf_op jit(solution)/shard_map/while/body/eval_jaxpr/kij,kjf->if/dot_general | solution.py:24
  399.0 4.1 gather_fusion.1
  403.1 4.7 %fusion.50 = f32[4,64,64]{2,1,0:T(8,128)S(1)} fusion(f32[4,64,64]{2,1,0:T(8,128)S(1)} %get-tuple-element.190, s32[]{:T(128)} %get-tuple-element.189, f32[64,64,64]{2,1,0:T(8,128)S(1)} %gather_fusion.1, f32[4,64,64,64]{1,2,3,0:T(8,128)} %get-tuple-element.197), kind=kOutput, calls=%fused_computation.19.clone.1 | convolution fusion | flops 201326592 | bytes 4228096 | tf_op jit(solution)/shard_map/while/body/eval_jaxpr/kij,kjf->if/dot_general | solution.py:24
  407.8 4.1 gather_fusion.1
  411.9 4.7 %fusion.50 = f32[4,64,64]{2,1,0:T(8,128)S(1)} fusion(f32[4,64,64]{2,1,0:T(8,128)S(1)} %get-tuple-element.190, s32[]{:T(128)} %get-tuple-element.189, f32[64,64,64]{2,1,0:T(8,128)S(1)} %gather_fusion.1, f32[4,64,64,64]{1,2,3,0:T(8,128)} %get-tuple-element.197), kind=kOutput, calls=%fused_computation.19.clone.1 | convolution fusion | flops 201326592 | bytes 4228096 | tf_op jit(solution)/shard_map/while/body/eval_jaxpr/kij,kjf->if/dot_general | solution.py:24
  416.6 0.7 copy.33
  (19 shorter events, 0.1 us)
Async XLA Ops:
  7.2 170.4 %all-gather.4.cloned.1.call-start = ((), (), s32[]{:S(2)}) async-start(), calls=%async_computation.1 | async-start | bytes 4259840 | tf_op jit(solution)/shard_map/all_gather | solution.py:38
  10.4 7.4 %copy-start = (s32[4,8]{1,0:T(4,128)S(1)}, s32[4,8]{1,0:T(4,128)}, u32[]{:S(2)}) copy-start(s32[4,8]{1,0:T(4,128)} %param.10) | copy-start | bytes 388
  10.4 63.3 %copy-start.1 = (s32[4]{0:T(128)S(1)}, s32[4]{0:T(128)}, u32[]{:S(2)}) copy-start(s32[4]{0:T(128)} %param.11) | copy-start | bytes 52
  10.4 63.4 %all-to-all-start = ((bf16[8,4,8,4096]{3,2,1,0:T(8,128)(2,1)}), bf16[8,4,8,4096]{3,2,1,0:T(8,128)(2,1)S(1)}, u32[]{:S(2)}, u32[]{:S(2)}) async-start(bf16[8,4,8,4096]{3,2,1,0:T(8,128)(2,1)} %stack.2), calls=%async_computation | async-start | bytes 4194304 | tf_op jit(solution)/shard_map/all_to_all | solution.py:33
  17.8 356.7 %all-gather.6.cloned.1.call-start = ((), (), s32[]{:S(2)}) async-start(), calls=%async_computation.2 | async-start | bytes 4259840 | tf_op jit(solution)/shard_map/all_gather | solution.py:40
Sparse Core Ops, SparseCore 0:
  12.3 165.1 all-gather.3
  220.4 154.0 all-gather.5
